TPU v7x, 32 devices: a whole 2x2x4 slice. The times are simulated.
32 devices in a mesh: section: 8 (over z, core), tensor: 4 (over y, x).
Axes of the slice: x: 2, y: 2, z: 4, core: 2. Of those that a mesh axis runs over, the one named last changes fastest.
Arguments:
- fwd_in: bfloat16 [8, 128, 2304], P('section', None, 'tensor'), may hold values from -6 to 6
- back_in: bfloat16 [8, 128, 2304], P('section', None, 'tensor'), may hold values from -0.59765625 to 0.59765625
- stash: bfloat16 [2, 8, 128, 2304], P(None, 'section', None, 'tensor'), may hold values from -6 to 6
- w_qkv: bfloat16 [8, 2304, 3, 4, 128], P('section', None, None, 'tensor'), may hold values from -0.125 to 0.125
- w_out: bfloat16 [8, 4, 128, 2304], P('section', 'tensor'), may hold values from -0.25 to 0.25
- norm_gain: bfloat16 [8, 2304], P('section'), may hold values from 0.25 to 1.75
- final_gain: bfloat16 [2304], replicated, may hold values from 0.25 to 1.75
- table: bfloat16 [8192, 2304], P(('section', 'tensor')), may hold values from -0.5625 to 0.5625
- ids: int32 [2, 128], replicated, may hold values from 0 to 8191
- back_ids: int32 [2, 128], replicated, may hold values from 0 to 8191
- targets: int32 [2, 128], replicated, may hold values from 0 to 8191
Outputs:
- fwd_out: bfloat16 [8, 128, 2304], P('section', None, 'tensor')
- back_out: bfloat16 [8, 128, 2304], P('section', None, 'tensor')
- table_grad: bfloat16 [8192, 2304], P(('section', 'tensor'))
- losses: float32 [2], replicated
All inputs are finite; a program needn't handle non-finite values.
Results may differ from a plain program's by a relative error of at most 0.035.
Values may be sent and summed in bfloat16 or wider, within the bound.
No kernel may reach another device: no remote copies, remote signals or barrier semaphores. Data moves between devices by JAX's collectives and lax.ppermute only.
A program may use at most 64 MiB of HBM per device.

v0:
```python
import math
import jax
import jax.numpy as jnp
from jax import lax
from jax.sharding import PartitionSpec as P

EPS = 1e-06
ATTN_CAP = 50.0
LOGIT_CAP = 30.0


def for_sending(x):

    def short(part):
        return part.astype(jnp.bfloat16) if part.dtype == jnp.float32 else part

    return jax.tree.map(short, x)


def passed_along(block, axis, distance):
    devices = range(lax.axis_size(axis))
    route = [(i - distance, i) for i in devices if i - distance in devices]
    return lax.ppermute(block, axis, route)


def broadcast(block, axis, holder):
    block = jnp.where(lax.axis_index(axis) == holder, block, jnp.zeros_like(block))
    return lax.psum(block, axis)


def widen(values):
    return jax.tree.map(
        lambda part, own: part.astype(own.dtype),
        lax.all_gather(for_sending(values), "tensor", axis=1, tiled=True),
        values,
    )


def sum_width(term):
    return lax.psum_scatter(
        term.astype(jnp.bfloat16), "tensor", scatter_dimension=1, tiled=True
    ).astype(jnp.float32)


def stat_width(values):
    return lax.psum(values, "tensor")


def sum_section(values):
    return jax.tree.map(
        lambda part: part.astype(jnp.float32), lax.psum(for_sending(values), "section")
    )


def pass_section(values, offset):
    return passed_along(values, "section", offset)


def feed(values, root):
    return broadcast(widen(values), "section", root)


def reduce_lookup(parts, width_pos, piece):
    summed = lax.psum(parts, ("section", "tensor"))
    return lax.dynamic_slice_in_dim(summed, width_pos * piece, piece, 1)


def row_scale(values):
    return lax.rsqrt(jnp.mean(values * values, axis=-1, keepdims=True) + EPS)


def attend(normed, weights):
    qkv = jnp.einsum("rd,dchk->chrk", normed, weights, preferred_element_type=jnp.float32).astype(
        jnp.bfloat16
    )
    query, keys, values = (qkv[0], qkv[1], qkv[2])
    length = normed.shape[0]
    scores = jnp.einsum(
        "hqk,hsk->hqs", query, keys, preferred_element_type=jnp.float32
    ) * query.shape[-1] ** (-0.5)
    capped = jnp.tanh(scores / ATTN_CAP)
    places = lax.iota(jnp.int32, length)
    causal = places[None, :] <= places[:, None]
    raised = jnp.where(causal[None], jnp.exp(ATTN_CAP * capped), 0.0)
    probs = (raised / jnp.sum(raised, axis=-1, keepdims=True)).astype(jnp.bfloat16)
    mixed = jnp.einsum("hqs,hsk->hqk", probs, values, preferred_element_type=jnp.float32).astype(
        jnp.bfloat16
    )
    return (query, keys, values, capped, probs, mixed)


def norm_back(xfull, xpiece, gpiece, dnorm, full_width):
    scale = row_scale(xfull)
    stat = stat_width(jnp.sum(xpiece * gpiece * dnorm, axis=1))
    return scale * gpiece * dnorm - xpiece * scale**3 * stat[:, None] / full_width


def body(
    fwd_in, back_in, stash, w_qkv, w_out, norm_gain, final_gain, table, ids, back_ids, targets
):
    section_pos = lax.axis_index("section")
    section_count = lax.axis_size("section")
    width_pos = lax.axis_index("tensor")
    width_count = lax.axis_size("tensor")
    acts = fwd_in[0]
    cots = back_in[0]
    rows, piece = acts.shape
    full_width = piece * width_count
    vocab_rows = table.shape[0]
    first_col = (section_pos * width_count + width_pos) * vocab_rows
    columns = first_col + lax.iota(jnp.int32, vocab_rows)
    emb_scale = math.sqrt(full_width)
    gain = norm_gain[0].astype(jnp.float32)
    gain_piece = lax.dynamic_slice_in_dim(gain, width_pos * piece, piece, 0)
    fgain = final_gain.astype(jnp.float32)
    fgain_piece = lax.dynamic_slice_in_dim(fgain, width_pos * piece, piece, 0)
    weights = w_qkv[0]
    outw = w_out[0]
    ticks = ids.shape[0]
    is_first = section_pos == 0
    is_last = section_pos == section_count - 1
    grad = jnp.zeros((vocab_rows, full_width), jnp.float32)
    losses = []
    previous = acts
    for tick in range(ticks):
        xfull = widen(acts).astype(jnp.float32)
        normed = (xfull * row_scale(xfull) * gain).astype(jnp.bfloat16)
        mixed = attend(normed, weights)[5]
        part = jnp.einsum("hrk,hkd->rd", mixed, outw, preferred_element_type=jnp.float32)
        outs_fwd = (acts.astype(jnp.float32) + sum_width(part)).astype(jnp.bfloat16)
        hidden = feed(outs_fwd, section_count - 1).astype(jnp.float32)
        hscale = row_scale(hidden)
        hnormed = (hidden * hscale * fgain).astype(jnp.bfloat16)
        raw = lax.dot_general(
            hnormed, table, (((1,), (1,)), ((), ())), preferred_element_type=jnp.float32
        )
        capped = jnp.tanh(raw / LOGIT_CAP)
        logits = LOGIT_CAP * capped
        raised = jnp.exp(logits)
        hit = targets[tick][:, None] == columns[None, :]
        tile_sums = stat_width(
            (jnp.sum(raised, axis=1), jnp.sum(jnp.where(hit, logits, 0.0), axis=1))
        )
        total, picked = sum_section(tile_sums)
        losses.append(jnp.mean(jnp.log(total) - picked))
        dlog = (
            (raised / total[:, None] - hit.astype(jnp.float32)) * (1.0 - capped * capped)
        ).astype(jnp.bfloat16)
        dpart = jnp.dot(dlog, table, preferred_element_type=jnp.float32)
        dhid = sum_section(sum_width(dpart))
        grad = grad + lax.dot_general(
            dlog, hnormed, (((0,), (0,)), ((), ())), preferred_element_type=jnp.float32
        )
        hpiece = lax.dynamic_slice_in_dim(hidden, width_pos * piece, piece, 1)
        cot_last = norm_back(hidden, hpiece, fgain_piece, dhid, full_width).astype(jnp.bfloat16)
        inputs_back = stash[tick, 0]
        if tick > 0:
            inputs_back = jnp.where(is_last, previous, inputs_back)
        bfull, upper = widen((inputs_back, cots))
        bfloat = bfull.astype(jnp.float32)
        bnormed = (bfloat * row_scale(bfloat) * gain).astype(jnp.bfloat16)
        query, keys, values, acapped, probs, amixed = attend(bnormed, weights)
        dmix = jnp.einsum("rd,hkd->hrk", upper, outw, preferred_element_type=jnp.float32).astype(
            jnp.bfloat16
        )
        dprob = jnp.einsum("hrk,hsk->hrs", dmix, values, preferred_element_type=jnp.float32)
        pfull = probs.astype(jnp.float32)
        dscore = pfull * (dprob - jnp.sum(dprob * pfull, axis=-1, keepdims=True))
        dlogit = (dscore * (1.0 - acapped * acapped) * query.shape[-1] ** (-0.5)).astype(
            jnp.bfloat16
        )
        dquery = jnp.einsum(
            "hqs,hsk->hqk", dlogit, keys, preferred_element_type=jnp.float32
        ).astype(jnp.bfloat16)
        dkeys = jnp.einsum(
            "hqs,hqk->hsk", dlogit, query, preferred_element_type=jnp.float32
        ).astype(jnp.bfloat16)
        dvalues = jnp.einsum(
            "hqs,hqk->hsk", probs, dmix, preferred_element_type=jnp.float32
        ).astype(jnp.bfloat16)
        stacked = jnp.stack([dquery, dkeys, dvalues])
        dterm = jnp.einsum("chrk,dchk->rd", stacked, weights, preferred_element_type=jnp.float32)
        dnorm = sum_width(dterm)
        bpiece = lax.dynamic_slice_in_dim(bfloat, width_pos * piece, piece, 1)
        dxf = norm_back(bfloat, bpiece, gain_piece, dnorm, full_width)
        outs_back = (cots.astype(jnp.float32) + dxf).astype(jnp.bfloat16)
        leaving = feed(outs_back, 0)
        back_hits = (back_ids[tick][:, None] == columns[None, :]).astype(jnp.bfloat16)
        look_grad = lax.dot_general(
            back_hits, leaving, (((0,), (0,)), ((), ())), preferred_element_type=jnp.float32
        )
        grad = grad + look_grad * emb_scale
        hits = (ids[tick][:, None] == columns[None, :]).astype(jnp.bfloat16)
        embedded = reduce_lookup(
            jnp.dot(hits, table, preferred_element_type=jnp.float32), width_pos, piece
        )
        entering = (embedded * emb_scale).astype(jnp.bfloat16)
        previous = acts
        acts = jnp.where(is_first, entering, pass_section(outs_fwd, 1))
        cots = jnp.where(is_last, cot_last, pass_section(outs_back, -1))
    return (acts[None], cots[None], grad.astype(jnp.bfloat16), jnp.stack(losses))


def solution(mesh):
    return jax.shard_map(
        body,
        mesh=mesh,
        in_specs=(
            P("section", None, "tensor"),
            P("section", None, "tensor"),
            P(None, "section", None, "tensor"),
            P("section", None, None, "tensor", None),
            P("section", "tensor", None, None),
            P("section", None),
            P(),
            P(("section", "tensor"), None),
            P(),
            P(),
            P(),
        ),
        out_specs=(
            P("section", None, "tensor"),
            P("section", None, "tensor"),
            P(("section", "tensor"), None),
            P(),
        ),
        check_vma=False,
    )
```

profile of v0, /device:TPU:0, one launch (start us, length us, event | category | flops | bytes accessed | tf_op | source)
XLA Modules:
  0.0 578.9 jit_solution(3762362679505095675)
XLA Ops:
  8.1 12.4 %all-gather = bf16[1,128,2304]{1,2,0:T(8,128)(2,1)S(1)} all-gather(bf16[1,128,576]{1,2,0:T(8,128)(2,1)} %param.11), channel_id=2, replica_groups=mesh['section'=8,'tensor'=4] {'tensor'}, dimensions={2}, use_global_device_ids=true | all-gather | bytes 737280 | tf_op jit(solution)/shard_map/all_gather | solution.py:34
  30.5 21.3 %reduce-scatter.7.cloned.1.call-done = bf16[128,576]{0,1:T(8,128)(2,1)} async-done(((bf16[128,2304]{0,1:T(8,128)(2,1)}), bf16[128,576]{0,1:T(8,128)(2,1)}) %reduce-scatter.7.cloned.1.call-update) | async-done | bytes 147472 | tf_op jit(solution)/shard_map/reduce_scatter | solution.py:40
  55.8 113.7 %all-reduce.14.cloned.1.call-done = (f32[128,2304]{0,1:T(8,128)}, f32[128,2304]{0,1:T(8,128)}) async-done(((f32[128,2304]{0,1:T(8,128)}, f32[128,2304]{0,1:T(8,128)}), (f32[128,2304]{0,1:T(8,128)}, f32[128,2304]{0,1:T(8,128)})) %all-reduce.14.cloned.1.call-update) | async-done | bytes 2359312 | tf_op jit(solution)/shard_map/psum | solution.py:64
  171.2 11.3 %all_gather.31 = bf16[128,2304]{0,1:T(8,128)(2,1)S(1)} all-gather(bf16[128,576]{0,1:T(8,128)(2,1)S(1)} %fusion.112), channel_id=1, replica_groups=mesh['section'=8,'tensor'=4] {'tensor'}, dimensions={1}, use_global_device_ids=true | all-gather | bytes 737280 | tf_op jit(solution)/shard_map/all_gather | solution.py:34
  188.2 10.5 %all_gather.33 = bf16[128,2304]{0,1:T(8,128)(2,1)S(1)} all-gather(bf16[128,576]{0,1:T(8,128)(2,1)} %add_convert_fusion.1), channel_id=1, replica_groups=mesh['section'=8,'tensor'=4] {'tensor'}, dimensions={1}, use_global_device_ids=true | all-gather | bytes 737280 | tf_op jit(solution)/shard_map/all_gather | solution.py:34
  199.5 13.0 %reduce-scatter.9.cloned.1.call-done = bf16[128,576]{0,1:T(8,128)(2,1)} async-done(((bf16[128,2304]{0,1:T(8,128)(2,1)}), bf16[128,576]{0,1:T(8,128)(2,1)}) %reduce-scatter.9.cloned.1.call-update) | async-done | bytes 147472 | tf_op jit(solution)/shard_map/reduce_scatter | solution.py:40
  214.2 10.2 %all_gather.32 = bf16[128,2304]{0,1:T(8,128)(2,1)S(1)} all-gather(bf16[128,576]{0,1:T(8,128)(2,1)S(1)} %add_convert_fusion), channel_id=1, replica_groups=mesh['section'=8,'tensor'=4] {'tensor'}, dimensions={1}, use_global_device_ids=true | all-gather | bytes 737280 | tf_op jit(solution)/shard_map/all_gather | solution.py:34
  228.3 11.7 %all-gather.2 = bf16[1,128,2304]{1,2,0:T(8,128)(2,1)} all-gather(bf16[1,128,576]{1,2,0:T(8,128)(2,1)} %param.12), channel_id=4, replica_groups=mesh['section'=8,'tensor'=4] {'tensor'}, dimensions={2}, use_global_device_ids=true | all-gather | bytes 737280 | tf_op jit(solution)/shard_map/all_gather | solution.py:34
  241.2 43.7 %all-reduce.20.cloned.1.call-done = (bf16[128,2304]{0,1:T(8,128)(2,1)}, bf16[128,2304]{0,1:T(8,128)(2,1)}) async-done(((bf16[128,2304]{0,1:T(8,128)(2,1)}, bf16[128,2304]{0,1:T(8,128)(2,1)}), (bf16[128,2304]{0,1:T(8,128)(2,1)}, bf16[128,2304]{0,1:T(8,128)(2,1)})) %all-reduce.20.cloned.1.call-update) | async-done | bytes 1179664 | tf_op jit(solution)/shard_map/psum | solution.py:28
  291.1 10.7 %all-reduce.3 = (bf16[128]{0:T(256)(128)(2,1)}, bf16[128]{0:T(256)(128)(2,1)}) all-reduce(f32[128]{0:T(128)} %get-tuple-element.5, f32[128]{0:T(128)} %get-tuple-element.10), channel_id=1, replica_groups=mesh['section'=8,'tensor'=4] {'tensor'}, use_global_device_ids=true, to_apply=%region_20.21 | all-reduce | flops 256 | bytes 1536 | tf_op jit(solution)/shard_map/psum | solution.py:46
  301.8 14.3 %all-reduce.5 = (bf16[128]{0:T(256)(128)(2,1)}, bf16[128]{0:T(256)(128)(2,1)}) all-reduce(bf16[128]{0:T(256)(128)(2,1)} %get-tuple-element.21, bf16[128]{0:T(256)(128)(2,1)} %get-tuple-element.20), channel_id=1, replica_groups=mesh['section'=8,'tensor'=4] {'section'}, use_global_device_ids=true, to_apply=%region_12.13 | all-reduce | flops 256 | bytes 1024 | tf_op jit(solution)/shard_map/psum | solution.py:51
  319.8 12.8 %all-gather.1 = bf16[1,1,128,2304]{2,3,1,0:T(8,128)(2,1)S(1)} all-gather(bf16[1,1,128,576]{2,3,1,0:T(8,128)(2,1)} %slice.70), channel_id=3, replica_groups=mesh['section'=8,'tensor'=4] {'tensor'}, dimensions={3}, use_global_device_ids=true | all-gather | bytes 737280 | tf_op jit(solution)/shard_map/all_gather | solution.py:34
  342.8 10.7 %all_gather.36 = bf16[128,2304]{0,1:T(8,128)(2,1)S(1)} all-gather(bf16[128,576]{0,1:T(8,128)(2,1)S(1)} %bitcast_select_fusion), channel_id=1, replica_groups=mesh['section'=8,'tensor'=4] {'tensor'}, dimensions={1}, use_global_device_ids=true | all-gather | bytes 737280 | tf_op jit(solution)/shard_map/all_gather | solution.py:34
  356.7 13.5 %reduce-scatter.13.cloned.1.call-done = bf16[128,576]{0,1:T(8,128)(2,1)} async-done(((bf16[128,2304]{0,1:T(8,128)(2,1)}), bf16[128,576]{0,1:T(8,128)(2,1)}) %reduce-scatter.13.cloned.1.call-update) | async-done | bytes 147472 | tf_op jit(solution)/shard_map/reduce_scatter | solution.py:40
  375.4 22.8 %reduce-scatter.15.cloned.1.call-done = bf16[128,576]{0,1:T(8,128)(2,1)} async-done(((bf16[128,2304]{0,1:T(8,128)(2,1)}), bf16[128,576]{0,1:T(8,128)(2,1)}) %reduce-scatter.15.cloned.1.call-update) | async-done | bytes 147472 | tf_op jit(solution)/shard_map/reduce_scatter | solution.py:40
  402.2 21.0 %all-reduce.18.cloned.1.call-done = (bf16[128,576]{0,1:T(8,128)(2,1)}, bf16[128,576]{0,1:T(8,128)(2,1)}) async-done(((bf16[128,576]{0,1:T(8,128)(2,1)}, bf16[128,576]{0,1:T(8,128)(2,1)}), (bf16[128,576]{0,1:T(8,128)(2,1)}, bf16[128,576]{0,1:T(8,128)(2,1)})) %all-reduce.18.cloned.1.call-update) | async-done | bytes 294928 | tf_op jit(solution)/shard_map/psum | solution.py:51
  425.2 10.5 %all-reduce.2 = (f32[128]{0:T(128)}, f32[128]{0:T(128)}) all-reduce(f32[128]{0:T(128)} %fusion.101, f32[128]{0:T(128)} %get-tuple-element.9), channel_id=1, replica_groups=mesh['section'=8,'tensor'=4] {'tensor'}, use_global_device_ids=true, to_apply=%region_31.32 | all-reduce | flops 256 | bytes 2048 | tf_op jit(solution)/shard_map/psum | solution.py:46
  444.5 11.0 %all_gather.37 = bf16[128,2304]{0,1:T(8,128)(2,1)S(1)} all-gather(bf16[128,576]{0,1:T(8,128)(2,1)S(1)} %fusion.113), channel_id=1, replica_groups=mesh['section'=8,'tensor'=4] {'tensor'}, dimensions={1}, use_global_device_ids=true | all-gather | bytes 737280 | tf_op jit(solution)/shard_map/all_gather | solution.py:34
  462.3 13.0 %all_gather.38 = bf16[128,2304]{0,1:T(8,128)(2,1)S(1)} all-gather(bf16[128,576]{0,1:T(8,128)(2,1)S(1)} %copy-done.18), channel_id=1, replica_groups=mesh['section'=8,'tensor'=4] {'tensor'}, dimensions={1}, use_global_device_ids=true | all-gather | bytes 737280 | tf_op jit(solution)/shard_map/all_gather | solution.py:34
  476.2 7.2 %reduce-scatter.17.cloned.1.call-done = bf16[128,576]{0,1:T(8,128)(2,1)} async-done(((bf16[128,2304]{0,1:T(8,128)(2,1)}), bf16[128,576]{0,1:T(8,128)(2,1)}) %reduce-scatter.17.cloned.1.call-update) | async-done | bytes 147472 | tf_op jit(solution)/shard_map/reduce_scatter | solution.py:40
  484.6 9.3 %all-reduce.1 = (f32[128]{0:T(128)S(1)}, f32[128]{0:T(128)S(1)}, bf16[128]{0:T(256)(128)(2,1)S(1)}, bf16[128]{0:T(256)(128)(2,1)S(1)}) all-reduce(f32[128]{0:T(128)S(1)} %fusion.105, f32[128]{0:T(128)S(1)} %copy-done.55, f32[128]{0:T(128)S(1)} %copy-done.63, f32[128]{0:T(128)S(1)} %copy-done.62), channel_id=1, replica_groups=mesh['section'=8,'tensor'=4] {'tensor'}, use_global_device_ids=true, to_apply=%region_37.38 | all-reduce | flops 512 | bytes 3584 | tf_op jit(solution)/shard_map/psum | solution.py:46
  495.1 10.6 %all_gather.39 = bf16[128,2304]{0,1:T(8,128)(2,1)S(1)} all-gather(bf16[128,576]{0,1:T(8,128)(2,1)S(1)} %fusion.104), channel_id=1, replica_groups=mesh['section'=8,'tensor'=4] {'tensor'}, dimensions={1}, use_global_device_ids=true | all-gather | bytes 737280 | tf_op jit(solution)/shard_map/all_gather | solution.py:34
  510.3 17.9 %all-reduce.4 = (bf16[128]{0:T(256)(128)(2,1)S(1)}, bf16[128]{0:T(256)(128)(2,1)S(1)}) all-reduce(bf16[128]{0:T(256)(128)(2,1)S(1)} %get-tuple-element.16, bf16[128]{0:T(256)(128)(2,1)S(1)} %get-tuple-element.17), channel_id=1, replica_groups=mesh['section'=8,'tensor'=4] {'section'}, use_global_device_ids=true, to_apply=%region_46.47 | all-reduce | flops 256 | bytes 1024 | tf_op jit(solution)/shard_map/psum | solution.py:51
  533.0 33.5 %all-reduce.16.cloned.1.call-done = (bf16[128,2304]{0,1:T(8,128)(2,1)}, bf16[128,2304]{0,1:T(8,128)(2,1)}) async-done(((bf16[128,2304]{0,1:T(8,128)(2,1)}, bf16[128,2304]{0,1:T(8,128)(2,1)}), (bf16[128,2304]{0,1:T(8,128)(2,1)}, bf16[128,2304]{0,1:T(8,128)(2,1)})) %all-reduce.16.cloned.1.call-update) | async-done | bytes 1179664 | tf_op jit(solution)/shard_map/psum | solution.py:28
  (245 shorter events, 94.5 us)
Async XLA Ops:
  8.0 43.8 %reduce-scatter.7.cloned.1.call-start = ((), (), s32[]{:S(2)}) async-start(), calls=%async_computation.6 | async-start | bytes 737280 | tf_op jit(solution)/shard_map/reduce_scatter | solution.py:40
  26.3 143.2 %all-reduce.14.cloned.1.call-start = ((), (), s32[]{:S(2)}) async-start(), calls=%async_computation.12 | async-start | bytes 4718592 | tf_op jit(solution)/shard_map/psum | solution.py:64
  26.4 310.4 %copy-start.30 = (s32[256]{0:T(256)}, s32[256]{0:T(256)S(1)}, u32[]{:S(2)}) copy-start(s32[256]{0:T(256)S(1)} %iota_add_fusion) | copy-start | bytes 3076
  30.5 182.1 %reduce-scatter.9.cloned.1.call-start = ((), (), s32[]{:S(2)}) async-start(), calls=%async_computation.7 | async-start | bytes 737280 | tf_op jit(solution)/shard_map/reduce_scatter | solution.py:40
  53.5 116.0 %collective-permute-start = (bf16[128,576]{0,1:T(8,128)(2,1)}, bf16[128,576]{0,1:T(8,128)(2,1)}, u32[]{:S(2)}, u32[]{:S(2)}) collective-permute-start(bf16[128,576]{0,1:T(8,128)(2,1)} %add_convert_fusion.1), channel_id=1, source_target_pairs={{0,4},{4,8},{8,12},{12,16},{16,20},{20,24},{24,28},{1,5},{5,9},{9,... | collective-permute-start | bytes 442376 | tf_op jit(solution)/shard_map/ppermute | solution.py:23
  188.1 96.8 %all-reduce.20.cloned.1.call-start = ((), (), s32[]{:S(2)}) async-start(), calls=%async_computation.15 | async-start | bytes 2359296 | tf_op jit(solution)/shard_map/psum | solution.py:28
  225.3 131.3 %reduce-scatter.11.cloned.1.call-start = ((), (), s32[]{:S(2)}) async-start(), calls=%async_computation.8 | async-start | bytes 737280 | tf_op jit(solution)/shard_map/reduce_scatter | solution.py:40
  319.8 50.3 %reduce-scatter.13.cloned.1.call-start = ((), (), s32[]{:S(2)}) async-start(), calls=%async_computation.9 | async-start | bytes 737280 | tf_op jit(solution)/shard_map/reduce_scatter | solution.py:40
  338.7 59.5 %reduce-scatter.15.cloned.1.call-start = ((), (), s32[]{:S(2)}) async-start(), calls=%async_computation.10 | async-start | bytes 737280 | tf_op jit(solution)/shard_map/reduce_scatter | solution.py:40
  342.7 80.5 %all-reduce.18.cloned.1.call-start = ((), (), s32[]{:S(2)}) async-start(), calls=%async_computation.14 | async-start | bytes 589824 | tf_op jit(solution)/shard_map/psum | solution.py:51
  370.2 113.2 %reduce-scatter.17.cloned.1.call-start = ((), (), s32[]{:S(2)}) async-start(), calls=%async_computation.11 | async-start | bytes 737280 | tf_op jit(solution)/shard_map/reduce_scatter | solution.py:40
  373.3 26.6 %copy-start.8 = (bf16[128,2304]{0,1:T(8,128)(2,1)S(1)}, bf16[128,2304]{0,1:T(8,128)(2,1)}, u32[]{:S(2)}) copy-start(bf16[128,2304]{0,1:T(8,128)(2,1)} %get-tuple-element.30) | copy-start | bytes 1769476
  374.2 69.0 %copy-start.33 = (f32[576]{0:T(1024)}, f32[576]{0:T(1024)S(1)}, u32[]{:S(2)}) copy-start(f32[576]{0:T(1024)S(1)} %dynamic_slice.28) | copy-start | bytes 6916
  375.3 25.8 %copy-start.6 = (bf16[128,2304]{0,1:T(8,128)(2,1)S(1)}, bf16[128,2304]{0,1:T(8,128)(2,1)}, u32[]{:S(2)}) copy-start(bf16[128,2304]{0,1:T(8,128)(2,1)} %get-tuple-element.31) | copy-start | bytes 1769476
  401.1 34.5 %copy-start.59 = (f32[128]{0:T(128)S(1)}, f32[128]{0:T(128)}, u32[]{:S(2)}) copy-start(f32[128]{0:T(128)} %copy-done.58) | copy-start | bytes 1540
  402.2 41.0 %copy-start.47 = (f32[128]{0:T(128)S(1)}, f32[128]{0:T(128)}, u32[]{:S(2)}) copy-start(f32[128]{0:T(128)} %copy-done.46) | copy-start | bytes 1540
  436.9 6.3 %collective-permute-start.2 = (bf16[128,576]{0,1:T(8,128)(2,1)S(1)}, bf16[128,576]{0,1:T(8,128)(2,1)S(1)}, u32[]{:S(2)}, u32[]{:S(2)}) collective-permute-start(bf16[128,576]{0,1:T(8,128)(2,1)S(1)} %fusion.100), channel_id=1, source_target_pairs={{4,0},{8,4},{12,8},{16,12},{20,16},{24,20},{28,24},{5,1},{9,5},{13... | collective-permute-start | bytes 442376 | tf_op jit(solution)/shard_map/ppermute | solution.py:23
  439.5 18.7 %collective-permute-start.1 = (bf16[128,576]{0,1:T(8,128)(2,1)}, bf16[128,576]{0,1:T(8,128)(2,1)}, u32[]{:S(2)}, u32[]{:S(2)}) collective-permute-start(bf16[128,576]{0,1:T(8,128)(2,1)} %copy-done.15), channel_id=1, source_target_pairs={{0,4},{4,8},{8,12},{12,16},{16,20},{20,24},{24,28},{1,5},{5,9},{9,... | collective-permute-start | bytes 442376 | tf_op jit(solution)/shard_map/ppermute | solution.py:23
  458.1 108.4 %all-reduce.16.cloned.1.call-start = ((), (), s32[]{:S(2)}) async-start(), calls=%async_computation.13 | async-start | bytes 2359296 | tf_op jit(solution)/shard_map/psum | solution.py:28
  462.2 31.6 %copy-start.12 = (bf16[128,576]{0,1:T(8,128)(2,1)S(1)}, bf16[128,576]{0,1:T(8,128)(2,1)}, u32[]{:S(2)}) copy-start(bf16[128,576]{0,1:T(8,128)(2,1)} %copy-done.11) | copy-start | bytes 442372
  462.2 31.6 %copy-start.57 = (f32[128]{0:T(128)S(1)}, f32[128]{0:T(128)}, u32[]{:S(2)}) copy-start(f32[128]{0:T(128)} %copy-done.56) | copy-start | bytes 1540
  462.3 31.6 %copy-start.64 = (f32[128]{0:T(128)S(1)}, f32[128]{0:T(128)}, u32[]{:S(2)}) copy-start(f32[128]{0:T(128)} %get-tuple-element.40) | copy-start | bytes 1540
  506.7 59.8 %copy-start.54 = (s32[128]{0:T(128)S(1)}, s32[128]{0:T(128)}, u32[]{:S(2)}) copy-start(s32[128]{0:T(128)} %get-tuple-element.33) | copy-start | bytes 1540
  509.0 22.2 %collective-permute-start.3 = (bf16[128,576]{0,1:T(8,128)(2,1)S(1)}, bf16[128,576]{0,1:T(8,128)(2,1)S(1)}, u32[]{:S(2)}, u32[]{:S(2)}) collective-permute-start(bf16[128,576]{0,1:T(8,128)(2,1)S(1)} %fusion.104), channel_id=1, source_target_pairs={{4,0},{8,4},{12,8},{16,12},{20,16},{24,20},{28,24},{5,1},{9,5},{13... | collective-permute-start | bytes 442376 | tf_op jit(solution)/shard_map/ppermute | solution.py:23
  (58 other events, 382.4 us)
Sparse Core Ops, SparseCore 0:
  26.4 25.3 reduce-scatter.6
  188.2 24.2 reduce-scatter.8
  319.9 22.2 reduce-scatter.10
  344.9 25.1 reduce-scatter.12
  373.1 25.1 reduce-scatter.14
  458.2 25.0 reduce-scatter.16
Sparse Core Ops, SparseCore 1:
  34.0 135.5 all-reduce.13
  225.4 59.5 all-reduce.19
  370.2 52.9 all-reduce.17
  506.7 59.8 all-reduce.15
where the time goes:
time: 580 us; the launch traced here: 579 us
  waiting for transfers between devices  290 us (50%)
  blocking collectives  177 us (31%)
  matrix products  41.2 us (7%)
  other arithmetic  33.3 us (6%)
  between operations  17.7 us (3%)
  local copies, waits for them, and re-layouts  10.9 us (2%)
  starting transfers between devices  8.97 us (2%)
    all_gather x10, blocking collectives, widen(): lax.all_gather(for_sending(values), 'tensor', axis=1, tiled=True)  114 us
    psum x1, waiting for transfers between devices, reduce_lookup(): summed = lax.psum(parts, ('section', 'tensor'))  114 us
    reduce_scatter x6, waiting for transfers between devices, sum_width(): lax.psum_scatter(term.astype(jnp.bfloat16), 'tensor', scatter_dimension=1...  77.8 us
    psum x2, waiting for transfers between devices, broadcast(): return lax.psum(block, axis)  77.3 us
    psum x2, blocking collectives, sum_section(): lax.psum(for_sending(values), 'section')  32.2 us
    psum x3, blocking collectives, stat_width(): return lax.psum(values, 'tensor')  30.4 us
    psum x1, waiting for transfers between devices, sum_section(): lax.psum(for_sending(values), 'section')  21 us
  transfers between devices with their start and end apart: 14, of which 9 were waited for; matrix products, arithmetic and copies ran while one was open for 8% of the time, Pallas kernels for 0%

commit v1 on v0

--- a/solution.py
+++ b/solution.py
@@ -61,7 +61,7 @@
 
 
 def reduce_lookup(parts, width_pos, piece):
-    summed = lax.psum(parts, ("section", "tensor"))
+    summed = lax.psum(lax.psum(parts, "tensor"), "section")
     return lax.dynamic_slice_in_dim(summed, width_pos * piece, piece, 1)
 
 

time: 580 us -> 630 us (1.086)
  waiting for transfers between devices: 290 us -> 338 us
    psum x1, waiting for transfers between devices: 21 us -> 51.6 us  [sum_section(): lax.psum(for_sending(values), 'section')]
    psum x1 -> x2, waiting for transfers between devices: 114 us -> 123 us  [reduce_lookup(): summed = lax.psum(lax.psum(parts, 'tensor'), 'section')]
    reduce_scatter x6, waiting for transfers between devices: 77.8 us -> 86.1 us  [sum_width(): lax.psum_scatter(term.astype(jnp.bfloat16), 'tensor', scatter_dimension=1...]
  transfers between devices with their start and end apart: 14 -> 15, of which waited for: 9 -> 11; matrix products, arithmetic and copies ran while one was open for 8% -> 8% of each run, Pallas kernels for 0% -> 0%
where the time goes in v1:
time: 630 us; the launch traced here: 629 us
  waiting for transfers between devices  338 us (54%)
  blocking collectives  178 us (28%)
  matrix products  43.3 us (7%)
  other arithmetic  32.7 us (5%)
  between operations  16 us (3%)
  local copies, waits for them, and re-layouts  11.6 us (2%)
  starting transfers between devices  8.99 us (1%)
    psum x2, waiting for transfers between devices, reduce_lookup(): summed = lax.psum(lax.psum(parts, 'tensor'), 'section')  123 us
    all_gather x10, blocking collectives, widen(): lax.all_gather(for_sending(values), 'tensor', axis=1, tiled=True)  115 us
    reduce_scatter x6, waiting for transfers between devices, sum_width(): lax.psum_scatter(term.astype(jnp.bfloat16), 'tensor', scatter_dimension=1...  86.1 us
    psum x2, waiting for transfers between devices, broadcast(): return lax.psum(block, axis)  77.1 us
    psum x1, waiting for transfers between devices, sum_section(): lax.psum(for_sending(values), 'section')  51.6 us
    psum x2, blocking collectives, sum_section(): lax.psum(for_sending(values), 'section')  32.4 us
    psum x3, blocking collectives, stat_width(): return lax.psum(values, 'tensor')  30.3 us
  transfers between devices with their start and end apart: 15, of which 11 were waited for; matrix products, arithmetic and copies ran while one was open for 8% of the time, Pallas kernels for 0%

profile of v1, /device:TPU:0, one launch (start us, length us, event | category | flops | bytes accessed | tf_op | source)
XLA Modules:
  0.0 628.7 jit_solution(16586042823150670020)
XLA Ops:
  13.7 14.8 %all-gather = bf16[1,128,2304]{1,2,0:T(8,128)(2,1)S(1)} all-gather(bf16[1,128,576]{1,2,0:T(8,128)(2,1)S(1)} %copy-done.10), channel_id=2, replica_groups=mesh['section'=8,'tensor'=4] {'tensor'}, dimensions={2}, use_global_device_ids=true | all-gather | bytes 737280 | tf_op jit(solution)/shard_map/all_gather | solution.py:34
  34.2 58.0 %all-reduce.18.cloned.1.call-done = (f32[128,2304]{0,1:T(8,128)}, f32[128,2304]{0,1:T(8,128)}) async-done(((f32[128,2304]{0,1:T(8,128)}, f32[128,2304]{0,1:T(8,128)}), (f32[128,2304]{0,1:T(8,128)}, f32[128,2304]{0,1:T(8,128)})) %all-reduce.18.cloned.1.call-update) | async-done | bytes 2359312 | tf_op jit(solution)/shard_map/psum | solution.py:64
  92.2 28.2 %reduce-scatter.7.cloned.1.call-done = bf16[128,576]{0,1:T(8,128)(2,1)} async-done(((bf16[128,2304]{0,1:T(8,128)(2,1)}), bf16[128,576]{0,1:T(8,128)(2,1)}) %reduce-scatter.7.cloned.1.call-update) | async-done | bytes 147472 | tf_op jit(solution)/shard_map/reduce_scatter | solution.py:40
  125.0 64.8 %all-reduce.16.cloned.1.call-done = (f32[128,2304]{0,1:T(8,128)}, f32[128,2304]{0,1:T(8,128)}) async-done(((f32[128,2304]{0,1:T(8,128)}, f32[128,2304]{0,1:T(8,128)}), (f32[128,2304]{0,1:T(8,128)}, f32[128,2304]{0,1:T(8,128)})) %all-reduce.16.cloned.1.call-update) | async-done | bytes 2359312 | tf_op jit(solution)/shard_map/psum | solution.py:64
  191.6 11.0 %all_gather.31 = bf16[128,2304]{0,1:T(8,128)(2,1)S(1)} all-gather(bf16[128,576]{0,1:T(8,128)(2,1)S(1)} %fusion.112), channel_id=1, replica_groups=mesh['section'=8,'tensor'=4] {'tensor'}, dimensions={1}, use_global_device_ids=true | all-gather | bytes 737280 | tf_op jit(solution)/shard_map/all_gather | solution.py:34
  208.2 10.2 %all_gather.33 = bf16[128,2304]{0,1:T(8,128)(2,1)S(1)} all-gather(bf16[128,576]{0,1:T(8,128)(2,1)} %add_convert_fusion.1), channel_id=1, replica_groups=mesh['section'=8,'tensor'=4] {'tensor'}, dimensions={1}, use_global_device_ids=true | all-gather | bytes 737280 | tf_op jit(solution)/shard_map/all_gather | solution.py:34
  219.3 13.0 %reduce-scatter.9.cloned.1.call-done = bf16[128,576]{0,1:T(8,128)(2,1)} async-done(((bf16[128,2304]{0,1:T(8,128)(2,1)}), bf16[128,576]{0,1:T(8,128)(2,1)}) %reduce-scatter.9.cloned.1.call-update) | async-done | bytes 147472 | tf_op jit(solution)/shard_map/reduce_scatter | solution.py:40
  234.0 10.2 %all_gather.32 = bf16[128,2304]{0,1:T(8,128)(2,1)S(1)} all-gather(bf16[128,576]{0,1:T(8,128)(2,1)S(1)} %add_convert_fusion), channel_id=1, replica_groups=mesh['section'=8,'tensor'=4] {'tensor'}, dimensions={1}, use_global_device_ids=true | all-gather | bytes 737280 | tf_op jit(solution)/shard_map/all_gather | solution.py:34
  248.0 11.7 %all-gather.2 = bf16[1,128,2304]{1,2,0:T(8,128)(2,1)} all-gather(bf16[1,128,576]{1,2,0:T(8,128)(2,1)} %param.12), channel_id=4, replica_groups=mesh['section'=8,'tensor'=4] {'tensor'}, dimensions={2}, use_global_device_ids=true | all-gather | bytes 737280 | tf_op jit(solution)/shard_map/all_gather | solution.py:34
  260.9 43.7 %all-reduce.24.cloned.1.call-done = (bf16[128,2304]{0,1:T(8,128)(2,1)}, bf16[128,2304]{0,1:T(8,128)(2,1)}) async-done(((bf16[128,2304]{0,1:T(8,128)(2,1)}, bf16[128,2304]{0,1:T(8,128)(2,1)}), (bf16[128,2304]{0,1:T(8,128)(2,1)}, bf16[128,2304]{0,1:T(8,128)(2,1)})) %all-reduce.24.cloned.1.call-update) | async-done | bytes 1179664 | tf_op jit(solution)/shard_map/psum | solution.py:28
  310.9 10.6 %all-reduce.3 = (bf16[128]{0:T(256)(128)(2,1)}, bf16[128]{0:T(256)(128)(2,1)}) all-reduce(f32[128]{0:T(128)} %get-tuple-element.5, f32[128]{0:T(128)} %get-tuple-element.10), channel_id=1, replica_groups=mesh['section'=8,'tensor'=4] {'tensor'}, use_global_device_ids=true, to_apply=%region_22.23 | all-reduce | flops 256 | bytes 1536 | tf_op jit(solution)/shard_map/psum | solution.py:46
  321.5 14.4 %all-reduce.6 = (bf16[128]{0:T(256)(128)(2,1)}, bf16[128]{0:T(256)(128)(2,1)}) all-reduce(bf16[128]{0:T(256)(128)(2,1)} %get-tuple-element.21, bf16[128]{0:T(256)(128)(2,1)} %get-tuple-element.20), channel_id=1, replica_groups=mesh['section'=8,'tensor'=4] {'section'}, use_global_device_ids=true, to_apply=%region_14.15 | all-reduce | flops 256 | bytes 1024 | tf_op jit(solution)/shard_map/psum | solution.py:51
  339.5 12.8 %all-gather.1 = bf16[1,1,128,2304]{2,3,1,0:T(8,128)(2,1)S(1)} all-gather(bf16[1,1,128,576]{2,3,1,0:T(8,128)(2,1)} %slice.70), channel_id=3, replica_groups=mesh['section'=8,'tensor'=4] {'tensor'}, dimensions={3}, use_global_device_ids=true | all-gather | bytes 737280 | tf_op jit(solution)/shard_map/all_gather | solution.py:34
  362.5 9.7 %all_gather.36 = bf16[128,2304]{0,1:T(8,128)(2,1)S(1)} all-gather(bf16[128,576]{0,1:T(8,128)(2,1)S(1)} %bitcast_select_fusion), channel_id=1, replica_groups=mesh['section'=8,'tensor'=4] {'tensor'}, dimensions={1}, use_global_device_ids=true | all-gather | bytes 737280 | tf_op jit(solution)/shard_map/all_gather | solution.py:34
  375.3 14.9 %reduce-scatter.13.cloned.1.call-done = bf16[128,576]{0,1:T(8,128)(2,1)} async-done(((bf16[128,2304]{0,1:T(8,128)(2,1)}), bf16[128,576]{0,1:T(8,128)(2,1)}) %reduce-scatter.13.cloned.1.call-update) | async-done | bytes 147472 | tf_op jit(solution)/shard_map/reduce_scatter | solution.py:40
  395.6 22.8 %reduce-scatter.15.cloned.1.call-done = bf16[128,576]{0,1:T(8,128)(2,1)} async-done(((bf16[128,2304]{0,1:T(8,128)(2,1)}), bf16[128,576]{0,1:T(8,128)(2,1)}) %reduce-scatter.15.cloned.1.call-update) | async-done | bytes 147472 | tf_op jit(solution)/shard_map/reduce_scatter | solution.py:40
  422.4 51.6 %all-reduce.22.cloned.1.call-done = (bf16[128,576]{0,1:T(8,128)(2,1)}, bf16[128,576]{0,1:T(8,128)(2,1)}) async-done(((bf16[128,576]{0,1:T(8,128)(2,1)}, bf16[128,576]{0,1:T(8,128)(2,1)}), (bf16[128,576]{0,1:T(8,128)(2,1)}, bf16[128,576]{0,1:T(8,128)(2,1)})) %all-reduce.22.cloned.1.call-update) | async-done | bytes 294928 | tf_op jit(solution)/shard_map/psum | solution.py:51
  475.8 10.5 %all-reduce.2 = (f32[128]{0:T(128)}, f32[128]{0:T(128)}) all-reduce(f32[128]{0:T(128)} %fusion.101, f32[128]{0:T(128)} %get-tuple-element.9), channel_id=1, replica_groups=mesh['section'=8,'tensor'=4] {'tensor'}, use_global_device_ids=true, to_apply=%region_33.34 | all-reduce | flops 256 | bytes 2048 | tf_op jit(solution)/shard_map/psum | solution.py:46
  495.1 11.0 %all_gather.37 = bf16[128,2304]{0,1:T(8,128)(2,1)S(1)} all-gather(bf16[128,576]{0,1:T(8,128)(2,1)S(1)} %fusion.113), channel_id=1, replica_groups=mesh['section'=8,'tensor'=4] {'tensor'}, dimensions={1}, use_global_device_ids=true | all-gather | bytes 737280 | tf_op jit(solution)/shard_map/all_gather | solution.py:34
  512.9 13.0 %all_gather.38 = bf16[128,2304]{0,1:T(8,128)(2,1)S(1)} all-gather(bf16[128,576]{0,1:T(8,128)(2,1)S(1)} %copy-done.19), channel_id=1, replica_groups=mesh['section'=8,'tensor'=4] {'tensor'}, dimensions={1}, use_global_device_ids=true | all-gather | bytes 737280 | tf_op jit(solution)/shard_map/all_gather | solution.py:34
  535.2 9.3 %all-reduce.1 = (f32[128]{0:T(128)S(1)}, f32[128]{0:T(128)S(1)}, bf16[128]{0:T(256)(128)(2,1)S(1)}, bf16[128]{0:T(256)(128)(2,1)S(1)}) all-reduce(f32[128]{0:T(128)S(1)} %fusion.105, f32[128]{0:T(128)S(1)} %copy-done.57, f32[128]{0:T(128)S(1)} %copy-done.65, f32[128]{0:T(128)S(1)} %copy-done.64), channel_id=1, replica_groups=mesh['section'=8,'tensor'=4] {'tensor'}, use_global_device_ids=true, to_apply=%region_39.40 | all-reduce | flops 512 | bytes 3584 | tf_op jit(solution)/shard_map/psum | solution.py:46
  545.7 10.6 %all_gather.39 = bf16[128,2304]{0,1:T(8,128)(2,1)S(1)} all-gather(bf16[128,576]{0,1:T(8,128)(2,1)S(1)} %fusion.104), channel_id=1, replica_groups=mesh['section'=8,'tensor'=4] {'tensor'}, dimensions={1}, use_global_device_ids=true | all-gather | bytes 737280 | tf_op jit(solution)/shard_map/all_gather | solution.py:34
  560.9 18.0 %all-reduce.5 = (bf16[128]{0:T(256)(128)(2,1)S(1)}, bf16[128]{0:T(256)(128)(2,1)S(1)}) all-reduce(bf16[128]{0:T(256)(128)(2,1)S(1)} %get-tuple-element.16, bf16[128]{0:T(256)(128)(2,1)S(1)} %get-tuple-element.17), channel_id=1, replica_groups=mesh['section'=8,'tensor'=4] {'section'}, use_global_device_ids=true, to_apply=%region_48.49 | all-reduce | flops 256 | bytes 1024 | tf_op jit(solution)/shard_map/psum | solution.py:51
  583.9 33.4 %all-reduce.20.cloned.1.call-done = (bf16[128,2304]{0,1:T(8,128)(2,1)}, bf16[128,2304]{0,1:T(8,128)(2,1)}) async-done(((bf16[128,2304]{0,1:T(8,128)(2,1)}, bf16[128,2304]{0,1:T(8,128)(2,1)}), (bf16[128,2304]{0,1:T(8,128)(2,1)}, bf16[128,2304]{0,1:T(8,128)(2,1)})) %all-reduce.20.cloned.1.call-update) | async-done | bytes 1179664 | tf_op jit(solution)/shard_map/psum | solution.py:28
  (252 shorter events, 104.6 us)
Async XLA Ops:
  7.2 85.0 %all-reduce.18.cloned.1.call-start = ((), (), s32[]{:S(2)}) async-start(), calls=%async_computation.13 | async-start | bytes 4718592 | tf_op jit(solution)/shard_map/psum | solution.py:64
  7.2 349.1 %copy-start.31 = (s32[256]{0:T(256)}, s32[256]{0:T(256)S(1)}, u32[]{:S(2)}) copy-start(s32[256]{0:T(256)S(1)} %iota_add_fusion) | copy-start | bytes 3076
  12.8 107.6 %reduce-scatter.7.cloned.1.call-start = ((), (), s32[]{:S(2)}) async-start(), calls=%async_computation.6 | async-start | bytes 737280 | tf_op jit(solution)/shard_map/reduce_scatter | solution.py:40
  34.1 155.7 %all-reduce.16.cloned.1.call-start = ((), (), s32[]{:S(2)}) async-start(), calls=%async_computation.12 | async-start | bytes 4718592 | tf_op jit(solution)/shard_map/psum | solution.py:64
  92.2 140.1 %reduce-scatter.9.cloned.1.call-start = ((), (), s32[]{:S(2)}) async-start(), calls=%async_computation.7 | async-start | bytes 737280 | tf_op jit(solution)/shard_map/reduce_scatter | solution.py:40
  122.1 3.0 collective-permute-start
  208.2 96.5 %all-reduce.24.cloned.1.call-start = ((), (), s32[]{:S(2)}) async-start(), calls=%async_computation.16 | async-start | bytes 2359296 | tf_op jit(solution)/shard_map/psum | solution.py:28
  245.0 130.3 %reduce-scatter.11.cloned.1.call-start = ((), (), s32[]{:S(2)}) async-start(), calls=%async_computation.8 | async-start | bytes 737280 | tf_op jit(solution)/shard_map/reduce_scatter | solution.py:40
  339.5 50.8 %reduce-scatter.13.cloned.1.call-start = ((), (), s32[]{:S(2)}) async-start(), calls=%async_computation.9 | async-start | bytes 737280 | tf_op jit(solution)/shard_map/reduce_scatter | solution.py:40
  358.4 60.1 %reduce-scatter.15.cloned.1.call-start = ((), (), s32[]{:S(2)}) async-start(), calls=%async_computation.10 | async-start | bytes 737280 | tf_op jit(solution)/shard_map/reduce_scatter | solution.py:40
  362.4 111.6 %all-reduce.22.cloned.1.call-start = ((), (), s32[]{:S(2)}) async-start(), calls=%async_computation.15 | async-start | bytes 589824 | tf_op jit(solution)/shard_map/psum | solution.py:51
  390.2 143.7 %reduce-scatter.17.cloned.1.call-start = ((), (), s32[]{:S(2)}) async-start(), calls=%async_computation.11 | async-start | bytes 737280 | tf_op jit(solution)/shard_map/reduce_scatter | solution.py:40
  393.5 26.6 %copy-start.8 = (bf16[128,2304]{0,1:T(8,128)(2,1)S(1)}, bf16[128,2304]{0,1:T(8,128)(2,1)}, u32[]{:S(2)}) copy-start(bf16[128,2304]{0,1:T(8,128)(2,1)} %get-tuple-element.32) | copy-start | bytes 1769476
  394.4 99.5 %copy-start.34 = (f32[576]{0:T(1024)}, f32[576]{0:T(1024)S(1)}, u32[]{:S(2)}) copy-start(f32[576]{0:T(1024)S(1)} %dynamic_slice.28) | copy-start | bytes 6916
  421.3 65.0 %copy-start.61 = (f32[128]{0:T(128)S(1)}, f32[128]{0:T(128)}, u32[]{:S(2)}) copy-start(f32[128]{0:T(128)} %copy-done.60) | copy-start | bytes 1540
  422.4 71.5 %copy-start.49 = (f32[128]{0:T(128)S(1)}, f32[128]{0:T(128)}, u32[]{:S(2)}) copy-start(f32[128]{0:T(128)} %copy-done.48) | copy-start | bytes 1540
  487.6 6.3 collective-permute-start.2
  490.1 18.6 %collective-permute-start.1 = (bf16[128,576]{0,1:T(8,128)(2,1)}, bf16[128,576]{0,1:T(8,128)(2,1)}, u32[]{:S(2)}, u32[]{:S(2)}) collective-permute-start(bf16[128,576]{0,1:T(8,128)(2,1)} %copy-done.16), channel_id=1, source_target_pairs={{0,4},{4,8},{8,12},{12,16},{16,20},{20,24},{24,28},{1,5},{5,9},{9,... | collective-permute-start | bytes 442376 | tf_op jit(solution)/shard_map/ppermute | solution.py:23
  508.7 108.6 %all-reduce.20.cloned.1.call-start = ((), (), s32[]{:S(2)}) async-start(), calls=%async_computation.14 | async-start | bytes 2359296 | tf_op jit(solution)/shard_map/psum | solution.py:28
  512.8 31.6 %copy-start.13 = (bf16[128,576]{0,1:T(8,128)(2,1)S(1)}, bf16[128,576]{0,1:T(8,128)(2,1)}, u32[]{:S(2)}) copy-start(bf16[128,576]{0,1:T(8,128)(2,1)} %copy-done.12) | copy-start | bytes 442372
  512.9 31.6 %copy-start.59 = (f32[128]{0:T(128)S(1)}, f32[128]{0:T(128)}, u32[]{:S(2)}) copy-start(f32[128]{0:T(128)} %copy-done.58) | copy-start | bytes 1540
  512.9 31.6 %copy-start.66 = (f32[128]{0:T(128)S(1)}, f32[128]{0:T(128)}, u32[]{:S(2)}) copy-start(f32[128]{0:T(128)} %get-tuple-element.42) | copy-start | bytes 1540
  557.3 60.1 %copy-start.56 = (s32[128]{0:T(128)S(1)}, s32[128]{0:T(128)}, u32[]{:S(2)}) copy-start(s32[128]{0:T(128)} %get-tuple-element.35) | copy-start | bytes 1540
  559.6 22.6 %collective-permute-start.3 = (bf16[128,576]{0,1:T(8,128)(2,1)S(1)}, bf16[128,576]{0,1:T(8,128)(2,1)S(1)}, u32[]{:S(2)}, u32[]{:S(2)}) collective-permute-start(bf16[128,576]{0,1:T(8,128)(2,1)S(1)} %fusion.104), channel_id=1, source_target_pairs={{4,0},{8,4},{12,8},{16,12},{20,16},{24,20},{28,24},{5,1},{9,5},{13... | collective-permute-start | bytes 442376 | tf_op jit(solution)/shard_map/ppermute | solution.py:23
  (61 other events, 437.3 us)
Sparse Core Ops, SparseCore 0:
  12.9 79.1 all-reduce.17
  95.3 25.0 reduce-scatter.6
  122.8 67.0 all-reduce.15
  208.3 23.9 reduce-scatter.8
  245.2 59.4 all-reduce.23
  339.6 22.1 reduce-scatter.10
  364.7 25.4 reduce-scatter.12
  393.3 25.0 reduce-scatter.14
  420.9 53.0 all-reduce.21
  508.9 25.0 reduce-scatter.16
  557.3 60.0 all-reduce.19
